TPU v7x, 32 devices: a whole 2x2x4 slice. The times are simulated.
32 devices in a mesh: occ: 4 (over y, core), aux: 8 (over z, x).
Axes of the slice: x: 2, y: 2, z: 4, core: 2. Of those that a mesh axis runs over, the one named last changes fastest.
Arguments:
- pair_ints: bfloat16 [16, 128, 20480], P(None, None, ('aux', 'occ')), may hold values from -110 to 110
- domain_len: int32 [4], replicated, may hold values from 1 to 4, as said below
- domain_blocks: int32 [4, 4], replicated, may hold values from 0 to 703
- slot_orbital: int32 [4], replicated, may hold values from 0 to 3, each once
- virt_energy: float32 [90112], replicated, may hold values from 0.1 to 3
- occ_energy: float32 [4], replicated, may hold values from -2 to -0.3
Outputs:
- projected: bfloat16 [4, 512, 20480], P('occ', None, 'aux')
Inputs may be any that keep to these rules, and one draw needn't show every extreme that they name: `domain_len`: some orbital has exactly 4 live blocks. `slot_orbital`: each orbital is owned by exactly one group.
All inputs are finite; a program needn't handle non-finite values.
Results may differ from a plain program's by a relative error of at most 0.001.
The roundings to bfloat16 on the way count: a program that leaves them out, or rounds other values in their place, can miss the bound.
Values may be sent and summed in bfloat16 or wider, within the bound.
A program may use at most 128 MiB of HBM per device.

v0:
```python
import jax
import jax.numpy as jnp
from jax import lax
from jax.sharding import PartitionSpec as P

LEVEL_RATIO = 0.5
EPSILON = 1e-05


def local(pair_ints, domain_len, domain_blocks, slot_orbital, virt_energy, occ_energy):
    orbitals = domain_len.shape[0]
    block_count = domain_blocks.shape[1]
    block_rows = pair_ints.shape[1]
    local_cols = pair_ints.shape[2]
    domain_size = block_count * block_rows
    slot_ids = jnp.arange(block_count, dtype=jnp.int32)
    ordered_len = jnp.take(domain_len, slot_orbital, axis=0)
    starts = (slot_orbital * block_count)[:, None] + slot_ids[None, :]
    live_mask = slot_ids[None, :] < ordered_len[:, None]
    flat_index = starts.reshape(-1)
    picked = jnp.take(pair_ints, flat_index, axis=0)
    picked = jnp.where(live_mask.reshape(-1)[:, None, None], picked, jnp.zeros_like(picked))
    padded = picked.reshape(orbitals, domain_size, local_cols)
    regrouped = lax.all_to_all(padded, "occ", split_axis=0, concat_axis=2, tiled=True)
    own_rows = regrouped[0]
    owner_group = lax.axis_index("occ")
    orbital = lax.dynamic_index_in_dim(slot_orbital, owner_group, 0, keepdims=False)
    partials = jnp.einsum("oac,obc->oab", padded, padded, preferred_element_type=jnp.float32)
    gram_part = lax.psum_scatter(
        partials.reshape(orbitals * domain_size, domain_size),
        ("occ", "aux"),
        scatter_dimension=0,
        tiled=True,
    )
    gram_sum = lax.all_gather(gram_part, "aux", axis=0, tiled=True)
    energy_table = virt_energy.reshape(-1, block_rows)
    blocks = lax.dynamic_index_in_dim(domain_blocks, orbital, 0, keepdims=False)
    energies = jnp.take(energy_table, blocks, axis=0).reshape(domain_size)
    occ_level = lax.dynamic_index_in_dim(occ_energy, orbital, 0, keepdims=False)
    denominator = energies[:, None] + energies[None, :] - 2.0 * occ_level
    amplitude = gram_sum / denominator
    length = lax.dynamic_index_in_dim(domain_len, orbital, 0, keepdims=False).astype(jnp.float32)
    level_shift = LEVEL_RATIO * (jnp.trace(amplitude) / (block_rows * length) + EPSILON)
    factor = jnp.linalg.cholesky(amplitude + level_shift * jnp.eye(domain_size, dtype=jnp.float32))
    solved = jax.scipy.linalg.cho_solve((factor, True), amplitude)
    projector = solved.T.astype(jnp.bfloat16)
    projected = jnp.dot(projector, own_rows, preferred_element_type=jnp.float32).astype(
        jnp.bfloat16
    )
    return projected[None]


def solution(mesh):
    placed = (P(None, None, ("aux", "occ")), P(), P(), P(), P(), P())
    return jax.shard_map(
        local, mesh=mesh, in_specs=placed, out_specs=P("occ", None, "aux"), check_vma=False
    )
```

profile of v0, /device:TPU:0, one launch (start us, length us, event | category | flops | bytes accessed | tf_op | source)
XLA Modules:
  0.0 390.7 jit_solution(3105162862275415704)
XLA Ops:
  6.5 0.8 compare_select_fusion.4
  7.4 1.3 gather_fusion
  8.6 0.7 and_select_fusion
  9.7 2.4 gather_fusion.1
  12.1 2.1 fusion.1
  14.2 3.8 fusion.62
  18.1 4.7 %all-to-all-start = ((bf16[4,512,640]{2,1,0:T(8,128)(2,1)}), bf16[4,512,640]{2,1,0:T(8,128)(2,1)}, u32[]{:S(2)}, u32[]{:S(2)}) async-start(bf16[4,512,640]{2,1,0:T(8,128)(2,1)} %copy-done.2), calls=%async_computation | async-start | bytes 5242880 | tf_op jit(solution)/shard_map/all_to_all | solution.py:24
  22.8 143.1 %reduce-scatter.4.cloned.1.call-done = f32[64,512]{1,0:T(8,128)} async-done(((f32[2048,512]{1,0:T(8,128)}), f32[64,512]{1,0:T(8,128)}) %reduce-scatter.4.cloned.1.call-update) | async-done | bytes 131088 | tf_op jit(solution)/shard_map/reduce_scatter | solution.py:29
  165.9 0.7 dynamic_slice.15
  168.7 0.7 dynamic_slice.18
  169.3 0.7 dynamic_slice.17
  170.7 1.5 gather_fusion.2
  173.1 4.8 %copy.58 = bf16[1,512,4,640]{1,3,2,0:T(8,128)(2,1)} copy(bf16[1,512,4,640]{3,1,2,0:T(8,128)(2,1)} %bitcast.23) | data formatting | bytes 5242880 | tf_op jit(solution)/shard_map/all_to_all | solution.py:24
  177.9 28.2 %all-gather.2.cloned.1.call-done = f32[512,512]{1,0:T(8,128)} async-done(((f32[64,512]{1,0:T(8,128)}), f32[512,512]{1,0:T(8,128)}) %all-gather.2.cloned.1.call-update) | async-done | bytes 1048592 | tf_op jit(solution)/shard_map/all_gather | solution.py:35
  206.2 2.6 copy.45
  208.8 3.2 select_reduce_fusion
  212.6 2.3 select_add_fusion
  215.0 2.5 copy.46
  217.5 1.8 fusion.2
  219.3 1.0 copy-done.5
  220.3 11.7 %cholesky.103 = f32[128,128]{1,0:T(8,128)S(1)} custom-call(f32[128,128]{1,0:T(8,128)S(1)} %cholesky.263), custom_call_target="Cholesky" | custom-call | tf_op jit(solution)/shard_map/jit(cholesky)/cholesky | solution.py:44
  232.0 9.8 %custom-call.34 = f32[1,128,128]{1,2,0:T(8,128)S(1)} custom-call(f32[1,128,128]{2,1,0:T(8,128)S(1)} %get-tuple-element.46), custom_call_target="InvertDiagBlocksLowerTriangular" | custom-call | tf_op jit(solution)/shard_map/jit(cholesky)/cholesky | solution.py:44
  241.9 1.2 fusion.32
  243.1 1.3 convolution_subtract_fusion.6
  244.4 11.7 %cholesky.215 = f32[128,128]{1,0:T(8,128)S(1)} custom-call(f32[128,128]{1,0:T(8,128)S(1)} %cholesky.267), custom_call_target="Cholesky" | custom-call | tf_op jit(solution)/shard_map/jit(cholesky)/cholesky | solution.py:44
  256.5 10.0 %custom-call.35 = f32[1,128,128]{1,2,0:T(8,128)S(1)} custom-call(f32[1,128,128]{2,1,0:T(8,128)S(1)} %get-tuple-element.44), custom_call_target="InvertDiagBlocksLowerTriangular" | custom-call | tf_op jit(solution)/shard_map/jit(cholesky)/cholesky | solution.py:44
  266.9 1.0 copy-done.3
  267.9 1.5 convolution_subtract_fusion.7
  269.4 11.7 %cholesky.236 = f32[128,128]{1,0:T(8,128)S(1)} custom-call(f32[128,128]{1,0:T(8,128)S(1)} %cholesky.272), custom_call_target="Cholesky" | custom-call | tf_op jit(solution)/shard_map/jit(cholesky)/cholesky | solution.py:44
  281.9 9.8 %custom-call.36 = f32[1,128,128]{1,2,0:T(8,128)S(1)} custom-call(f32[1,128,128]{2,1,0:T(8,128)S(1)} %get-tuple-element.42), custom_call_target="InvertDiagBlocksLowerTriangular" | custom-call | tf_op jit(solution)/shard_map/jit(cholesky)/cholesky | solution.py:44
  291.7 1.0 convolution_dynamic-update-slice_fusion.1
  292.7 1.6 convolution_subtract_fusion.8
  294.2 11.9 %cholesky.253 = f32[128,128]{1,0:T(8,128)S(1)} custom-call(f32[128,128]{1,0:T(8,128)S(1)} %convolution_subtract_fusion.8), custom_call_target="Cholesky" | custom-call | tf_op jit(solution)/shard_map/jit(cholesky)/cholesky | solution.py:44
  306.9 0.7 compare_reduce_fusion.3
  307.6 0.7 compare_reduce_fusion.1
  308.3 0.7 compare_reduce_fusion
  312.1 2.4 select_select_fusion
  314.5 14.2 %while.1 = (s32[]{:T(128)}, f32[512,512]{0,1:T(8,128)}, s32[4,2]{0,1:T(2,128)S(1)}, f32[4,128,128]{2,1,0:T(8,128)}, s32[]{:T(128)}) while((s32[]{:T(128)}, f32[512,512]{0,1:T(8,128)}, s32[4,2]{0,1:T(2,128)S(1)}, f32[4,128,128]{2,1,0:T(8,128)}, s32[]{:T(128)}) %tuple.32), condition=%wide.while_cond, body=%wide.while_body.sunk | while | flops 2 | bytes 393829 | solution.py:45
  315.1 2.2 dynamic-slice.7
  318.7 2.2 dynamic-slice.7
  322.2 2.2 dynamic-slice.7
  325.8 2.2 dynamic-slice.7
  328.7 40.1 %custom-call.37 = f32[4,128,128]{1,2,0:T(8,128)S(1)} custom-call(f32[4,128,128]{2,1,0:T(8,128)} %get-tuple-element.12), custom_call_target="InvertDiagBlocksLowerTriangular" | custom-call | tf_op jit(solution)/shard_map/jit(_cho_solve)/triangular_solve | solution.py:45
  368.8 1.5 fusion.26
  370.3 1.6 convolution_subtract_fusion.3
  372.3 2.0 convolution_subtract_fusion.2
  374.8 2.4 convolution_subtract_fusion.5
  380.6 3.1 fusion
  (85 shorter events, 13.2 us)
Async XLA Ops:
  6.5 3.2 copy-start
  6.5 159.3 %reduce-scatter.4.cloned.1.call-start = ((), (), s32[]{:S(2)}) async-start(), calls=%async_computation.3 | async-start | bytes 4325376 | tf_op jit(solution)/shard_map/reduce_scatter | solution.py:29
  14.2 3.8 copy-start.2
  18.0 147.9 %copy-start.7 = (s32[4]{0:T(128)S(1)}, s32[4]{0:T(128)}, u32[]{:S(2)}) copy-start(s32[4]{0:T(128)} %param.9) | copy-start | bytes 52
  18.0 150.6 %copy-start.1 = (s32[4]{0:T(128)S(1)}, s32[4]{0:T(128)}, u32[]{:S(2)}) copy-start(s32[4]{0:T(128)} %param.7) | copy-start | bytes 52
  18.0 151.3 %copy-start.9 = (f32[4]{0:T(128)S(1)}, f32[4]{0:T(128)}, u32[]{:S(2)}) copy-start(f32[4]{0:T(128)} %param.11) | copy-start | bytes 52
  18.0 152.6 %copy-start.8 = (s32[4,4]{1,0:T(4,128)S(1)}, s32[4,4]{1,0:T(4,128)}, u32[]{:S(2)}) copy-start(s32[4,4]{1,0:T(4,128)} %param.8) | copy-start | bytes 196
  18.1 155.0 %all-to-all-start = ((bf16[4,512,640]{2,1,0:T(8,128)(2,1)}), bf16[4,512,640]{2,1,0:T(8,128)(2,1)}, u32[]{:S(2)}, u32[]{:S(2)}) async-start(bf16[4,512,640]{2,1,0:T(8,128)(2,1)} %copy-done.2), calls=%async_computation | async-start | bytes 5242880 | tf_op jit(solution)/shard_map/all_to_all | solution.py:24
  22.8 183.4 %all-gather.2.cloned.1.call-start = ((), (), s32[]{:S(2)}) async-start(), calls=%async_computation.2 | async-start | bytes 1179648 | tf_op jit(solution)/shard_map/all_gather | solution.py:35
  219.3 1.0 copy-start.5
  266.9 1.0 copy-start.3
  368.8 5.9 %copy-start.4 = (f32[512,512]{0,1:T(8,128)S(1)}, f32[512,512]{0,1:T(8,128)}, u32[]{:S(2)}) copy-start(f32[512,512]{0,1:T(8,128)} %get-tuple-element.107) | copy-start | bytes 3145732
  378.0 2.6 copy-start.6
Sparse Core Ops, SparseCore 0:
  18.1 147.6 reduce-scatter.3
  168.0 38.1 all-gather.1
where the time goes:
time: 394 us; the launch traced here: 391 us
  waiting for transfers between devices  171 us (43%)
  other arithmetic  133 us (34%)
  local copies, waits for them, and re-layouts  35.5 us (9%)
  matrix products  25.2 us (6%)
  between operations  20.8 us (5%)
  starting transfers between devices  4.74 us (1%)
    reduce_scatter x1, waiting for transfers between devices, local(): lax.psum_scatter(partials.reshape(orbitals * domain_size, domain_size), (...  143 us
    another operation x15, other arithmetic, local(): jnp.linalg.cholesky(amplitude + level_shift * jnp.eye(domain_size, dtype=...  79.4 us
    another operation x3, other arithmetic, local(): solved = jax.scipy.linalg.cho_solve((factor, True), amplitude)  42.5 us
    all_gather x1, waiting for transfers between devices, local(): gram_sum = lax.all_gather(gram_part, 'aux', axis=0, tiled=True)  28.2 us
    another operation x20, local copies, waits for them, and re-layouts  14.2 us
    another operation x14, matrix products, local(): solved = jax.scipy.linalg.cho_solve((factor, True), amplitude)  11.6 us
  transfers between devices with their start and end apart: 3, of which 2 were waited for; matrix products, arithmetic and copies ran while one was open for 2% of the time, Pallas kernels for 0%

commit v1 on v0

--- a/solution.py
+++ b/solution.py
@@ -32,7 +32,12 @@
         scatter_dimension=0,
         tiled=True,
     )
-    gram_sum = lax.all_gather(gram_part, "aux", axis=0, tiled=True)
+    ring = [gram_part]
+    for hop in range(7):
+        ring.append(lax.ppermute(ring[-1], "aux", [(dev, (dev + 1) % 8) for dev in range(8)]))
+    gram_sum = jnp.roll(
+        jnp.concatenate(ring[::-1], axis=0), (lax.axis_index("aux") + 1) * ring[0].shape[0], axis=0
+    )
     energy_table = virt_energy.reshape(-1, block_rows)
     blocks = lax.dynamic_index_in_dim(domain_blocks, orbital, 0, keepdims=False)
     energies = jnp.take(energy_table, blocks, axis=0).reshape(domain_size)

time: 394 us -> 432 us (1.096)
  waiting for transfers between devices: 171 us -> 205 us
    unnamed x2, waiting for transfers between devices: 0.03 us -> 143 us
    reduce_scatter x1 -> x0, waiting for transfers between devices: 143 us -> none  [local(): lax.psum_scatter(partials.reshape(orbitals * domain_size, domain_size), (...]
    ppermute x0 -> x7, waiting for transfers between devices: none -> 61.4 us  [local(): lax.ppermute(ring[-1], 'aux', [(dev, (dev + 1) % 8) for dev in range(8)])]
    all_gather x1 -> x0, waiting for transfers between devices: 28.2 us -> none  [local(): gram_sum = lax.all_gather(gram_part, 'aux', axis=0, tiled=True)]
    concatenate x0 -> x1, local copies, waits for them, and re-layouts: none -> 4.81 us  [local(): jnp.roll(jnp.concatenate(ring[::-1], axis=0), (lax.axis_index('aux') + 1)...]
  transfers between devices with their start and end apart: 3 -> 9, of which waited for: 2 -> 8; matrix products, arithmetic and copies ran while one was open for 2% -> 2% of each run, Pallas kernels for 0% -> 0%
where the time goes in v1:
time: 432 us; the launch traced here: 427 us
  waiting for transfers between devices  205 us (47%)
  other arithmetic  133 us (31%)
  local copies, waits for them, and re-layouts  39.2 us (9%)
  matrix products  25 us (6%)
  between operations  20.2 us (5%)
  starting transfers between devices  4.76 us (1%)
    unnamed x2, waiting for transfers between devices  143 us
    another operation x15, other arithmetic, local(): jnp.linalg.cholesky(amplitude + level_shift * jnp.eye(domain_size, dtype=...  79.4 us
    ppermute x7, waiting for transfers between devices, local(): lax.ppermute(ring[-1], 'aux', [(dev, (dev + 1) % 8) for dev in range(8)])  61.4 us
    another operation x3, other arithmetic, local(): solved = jax.scipy.linalg.cho_solve((factor, True), amplitude)  42.5 us
    another operation x20, local copies, waits for them, and re-layouts  14.4 us
    another operation x14, matrix products, local(): solved = jax.scipy.linalg.cho_solve((factor, True), amplitude)  11.5 us
  transfers between devices with their start and end apart: 9, of which 8 were waited for; matrix products, arithmetic and copies ran while one was open for 2% of the time, Pallas kernels for 0%

profile of v1, /device:TPU:0, one launch (start us, length us, event | category | flops | bytes accessed | tf_op | source)
XLA Modules:
  0.0 427.2 jit_solution(6648733664944130824)
XLA Ops:
  7.4 1.3 gather_fusion
  9.7 2.4 gather_fusion.1
  12.1 2.1 fusion.1
  14.2 3.8 fusion.65
  18.1 4.7 %all-to-all-start = ((bf16[4,512,640]{2,1,0:T(8,128)(2,1)}), bf16[4,512,640]{2,1,0:T(8,128)(2,1)}, u32[]{:S(2)}, u32[]{:S(2)}) async-start(bf16[4,512,640]{2,1,0:T(8,128)(2,1)} %copy-done.2), calls=%async_computation | async-start | bytes 5242880 | tf_op jit(solution)/shard_map/all_to_all | solution.py:24
  22.8 143.3 %reduce-scatter.4.cloned.1.call-done = f32[64,512]{1,0:T(8,128)} async-done(((f32[2048,512]{1,0:T(8,128)}), f32[64,512]{1,0:T(8,128)}) %reduce-scatter.4.cloned.1.call-update) | async-done | bytes 131088
  166.0 1.0 copy.63
  167.1 9.1 %collective-permute-done = f32[64,512]{0,1:T(8,128)S(1)} collective-permute-done((f32[64,512]{0,1:T(8,128)S(1)}, f32[64,512]{0,1:T(8,128)S(1)}, u32[]{:S(2)}, u32[]{:S(2)}) %collective-permute-start) | collective-permute-done | bytes 131104 | tf_op jit(solution)/shard_map/ppermute | solution.py:37
  176.2 10.1 %collective-permute-done.1 = f32[64,512]{0,1:T(8,128)S(1)} collective-permute-done((f32[64,512]{0,1:T(8,128)S(1)}, f32[64,512]{0,1:T(8,128)S(1)}, u32[]{:S(2)}, u32[]{:S(2)}) %collective-permute-start.1) | collective-permute-done | bytes 131104 | tf_op jit(solution)/shard_map/ppermute | solution.py:37
  186.3 10.5 %collective-permute-done.2 = f32[64,512]{0,1:T(8,128)S(1)} collective-permute-done((f32[64,512]{0,1:T(8,128)S(1)}, f32[64,512]{0,1:T(8,128)S(1)}, u32[]{:S(2)}, u32[]{:S(2)}) %collective-permute-start.2) | collective-permute-done | bytes 131104 | tf_op jit(solution)/shard_map/ppermute | solution.py:37
  197.5 11.8 %collective-permute-done.3 = f32[64,512]{0,1:T(8,128)} collective-permute-done((f32[64,512]{0,1:T(8,128)S(1)}, f32[64,512]{0,1:T(8,128)}, u32[]{:S(2)}, u32[]{:S(2)}) %collective-permute-start.3) | collective-permute-done | bytes 131104 | tf_op jit(solution)/shard_map/ppermute | solution.py:37
  211.6 8.8 %collective-permute-done.4 = f32[64,512]{0,1:T(8,128)} collective-permute-done((f32[64,512]{0,1:T(8,128)}, f32[64,512]{0,1:T(8,128)}, u32[]{:S(2)}, u32[]{:S(2)}) %collective-permute-start.4) | collective-permute-done | bytes 131104 | tf_op jit(solution)/shard_map/ppermute | solution.py:37
  220.5 1.5 gather_fusion.2
  222.0 8.7 %collective-permute-done.5 = f32[64,512]{0,1:T(8,128)} collective-permute-done((f32[64,512]{0,1:T(8,128)}, f32[64,512]{0,1:T(8,128)}, u32[]{:S(2)}, u32[]{:S(2)}) %collective-permute-start.5) | collective-permute-done | bytes 131104 | tf_op jit(solution)/shard_map/ppermute | solution.py:37
  233.4 4.4 %copy.56 = bf16[1,512,4,640]{1,3,2,0:T(8,128)(2,1)} copy(bf16[1,512,4,640]{3,1,2,0:T(8,128)(2,1)} %bitcast.23) | data formatting | bytes 5242880 | tf_op jit(solution)/shard_map/all_to_all | solution.py:24
  237.7 2.4 collective-permute-done.6
  240.1 4.8 %concatenate.29 = f32[1024,512]{0,1:T(8,128)} concatenate(f32[64,512]{0,1:T(8,128)} %collective-permute-done.6, f32[64,512]{0,1:T(8,128)} %collective-permute-done.5, f32[64,512]{0,1:T(8,128)} %collective-permute-done.4, f32[64,512]{0,1:T(8,128)} %collective-permute-done.3, f32[64,512]{0,1:T(8,128)} %copy-done.8, f32[64,512]{0,1:T(8,128)S(1)} %collective-permute-done.1, ...), dimensions={0} | concatenate | bytes 4194304 | tf_op jit(solution)/shard_map/jit(_roll_dynamic)/concatenate | solution.py:38
  244.9 3.4 select_reduce_fusion
  249.0 2.3 select_add_fusion
  251.3 2.6 copy.44
  253.9 1.8 fusion.2
  255.7 1.0 copy-done.6
  256.6 11.7 %cholesky.103 = f32[128,128]{1,0:T(8,128)S(1)} custom-call(f32[128,128]{1,0:T(8,128)S(1)} %cholesky.263), custom_call_target="Cholesky" | custom-call | tf_op jit(solution)/shard_map/jit(cholesky)/cholesky | solution.py:49
  268.4 9.8 %custom-call.34 = f32[1,128,128]{1,2,0:T(8,128)S(1)} custom-call(f32[1,128,128]{2,1,0:T(8,128)S(1)} %get-tuple-element.46), custom_call_target="InvertDiagBlocksLowerTriangular" | custom-call | tf_op jit(solution)/shard_map/jit(cholesky)/cholesky | solution.py:49
  278.2 1.2 fusion.37
  279.4 1.3 convolution_subtract_fusion.3
  280.7 11.7 %cholesky.215 = f32[128,128]{1,0:T(8,128)S(1)} custom-call(f32[128,128]{1,0:T(8,128)S(1)} %cholesky.267), custom_call_target="Cholesky" | custom-call | tf_op jit(solution)/shard_map/jit(cholesky)/cholesky | solution.py:49
  292.8 10.0 %custom-call.35 = f32[1,128,128]{1,2,0:T(8,128)S(1)} custom-call(f32[1,128,128]{2,1,0:T(8,128)S(1)} %get-tuple-element.44), custom_call_target="InvertDiagBlocksLowerTriangular" | custom-call | tf_op jit(solution)/shard_map/jit(cholesky)/cholesky | solution.py:49
  303.3 1.0 copy-done.4
  304.3 1.5 convolution_subtract_fusion.4
  305.8 11.7 %cholesky.236 = f32[128,128]{1,0:T(8,128)S(1)} custom-call(f32[128,128]{1,0:T(8,128)S(1)} %cholesky.272), custom_call_target="Cholesky" | custom-call | tf_op jit(solution)/shard_map/jit(cholesky)/cholesky | solution.py:49
  318.3 9.8 %custom-call.36 = f32[1,128,128]{1,2,0:T(8,128)S(1)} custom-call(f32[1,128,128]{2,1,0:T(8,128)S(1)} %get-tuple-element.42), custom_call_target="InvertDiagBlocksLowerTriangular" | custom-call | tf_op jit(solution)/shard_map/jit(cholesky)/cholesky | solution.py:49
  328.1 0.9 convolution_dynamic-update-slice_fusion.1
  329.0 1.5 convolution_subtract_fusion.5
  330.5 11.9 %cholesky.253 = f32[128,128]{1,0:T(8,128)S(1)} custom-call(f32[128,128]{1,0:T(8,128)S(1)} %convolution_subtract_fusion.5), custom_call_target="Cholesky" | custom-call | tf_op jit(solution)/shard_map/jit(cholesky)/cholesky | solution.py:49
  348.4 2.3 select_select_fusion
  350.8 14.5 %while.1 = (s32[]{:T(128)}, f32[512,512]{0,1:T(8,128)}, s32[4,2]{0,1:T(2,128)S(1)}, f32[4,128,128]{2,1,0:T(8,128)}, s32[]{:T(128)}) while((s32[]{:T(128)}, f32[512,512]{0,1:T(8,128)}, s32[4,2]{0,1:T(2,128)S(1)}, f32[4,128,128]{2,1,0:T(8,128)}, s32[]{:T(128)}) %tuple.32), condition=%wide.while_cond, body=%wide.while_body.sunk | while | flops 2 | bytes 393829 | solution.py:50
  351.4 2.3 dynamic-slice.7
  355.0 2.3 dynamic-slice.7
  358.7 2.3 dynamic-slice.7
  362.3 2.2 dynamic-slice.7
  365.2 40.1 %custom-call.37 = f32[4,128,128]{1,2,0:T(8,128)S(1)} custom-call(f32[4,128,128]{2,1,0:T(8,128)} %get-tuple-element.12), custom_call_target="InvertDiagBlocksLowerTriangular" | custom-call | tf_op jit(solution)/shard_map/jit(_cho_solve)/triangular_solve | solution.py:50
  405.4 1.5 fusion.31
  406.9 1.4 fusion.44
  408.4 1.4 fusion.30
  409.7 1.9 fusion.14
  412.1 1.5 fusion.3
  417.0 3.1 fusion
  (101 shorter events, 19.0 us)
Async XLA Ops:
  6.5 3.2 copy-start
  6.5 159.5 %reduce-scatter.4.cloned.1.call-start = ((), (), s32[]{:S(2)}) async-start(), calls=%async_computation.2 | async-start | bytes 4325376
  14.2 3.8 copy-start.2
  18.0 191.3 %copy-start.9 = (s32[4]{0:T(128)S(1)}, s32[4]{0:T(128)}, u32[]{:S(2)}) copy-start(s32[4]{0:T(128)} %param.9) | copy-start | bytes 52
  18.0 193.6 %copy-start.10 = (s32[4,4]{1,0:T(4,128)S(1)}, s32[4,4]{1,0:T(4,128)}, u32[]{:S(2)}) copy-start(s32[4,4]{1,0:T(4,128)} %param.8) | copy-start | bytes 196
  18.0 212.8 %copy-start.1 = (s32[4]{0:T(128)S(1)}, s32[4]{0:T(128)}, u32[]{:S(2)}) copy-start(s32[4]{0:T(128)} %param.7) | copy-start | bytes 52
  18.1 213.4 %copy-start.11 = (f32[4]{0:T(128)S(1)}, f32[4]{0:T(128)}, u32[]{:S(2)}) copy-start(f32[4]{0:T(128)} %param.11) | copy-start | bytes 52
  18.1 215.3 %all-to-all-start = ((bf16[4,512,640]{2,1,0:T(8,128)(2,1)}), bf16[4,512,640]{2,1,0:T(8,128)(2,1)}, u32[]{:S(2)}, u32[]{:S(2)}) async-start(bf16[4,512,640]{2,1,0:T(8,128)(2,1)} %copy-done.2), calls=%async_computation | async-start | bytes 5242880 | tf_op jit(solution)/shard_map/all_to_all | solution.py:24
  167.1 9.1 %collective-permute-start = (f32[64,512]{0,1:T(8,128)S(1)}, f32[64,512]{0,1:T(8,128)S(1)}, u32[]{:S(2)}, u32[]{:S(2)}) collective-permute-start(f32[64,512]{0,1:T(8,128)S(1)} %copy.63), channel_id=1, source_target_pairs={{0,1},{1,2},{2,3},{3,4},{4,5},{5,6},{6,7},{7,0},{8,9},{9,10},{10,1... | collective-permute-start | bytes 393224 | tf_op jit(solution)/shard_map/ppermute | solution.py:37
  176.2 10.1 %collective-permute-start.1 = (f32[64,512]{0,1:T(8,128)S(1)}, f32[64,512]{0,1:T(8,128)S(1)}, u32[]{:S(2)}, u32[]{:S(2)}) collective-permute-start(f32[64,512]{0,1:T(8,128)S(1)} %collective-permute-done), channel_id=1, source_target_pairs={{0,1},{1,2},{2,3},{3,4},{4,5},{5,6},{6,7},{7,0},{8,9},{9,10},{10,1... | collective-permute-start | bytes 393224 | tf_op jit(solution)/shard_map/ppermute | solution.py:37
  186.3 10.6 %collective-permute-start.2 = (f32[64,512]{0,1:T(8,128)S(1)}, f32[64,512]{0,1:T(8,128)S(1)}, u32[]{:S(2)}, u32[]{:S(2)}) collective-permute-start(f32[64,512]{0,1:T(8,128)S(1)} %collective-permute-done.1), channel_id=1, source_target_pairs={{0,1},{1,2},{2,3},{3,4},{4,5},{5,6},{6,7},{7,0},{8,9},{9,10},{10,1... | collective-permute-start | bytes 393224 | tf_op jit(solution)/shard_map/ppermute | solution.py:37
  196.8 0.7 copy-start.8
  197.5 11.8 %collective-permute-start.3 = (f32[64,512]{0,1:T(8,128)S(1)}, f32[64,512]{0,1:T(8,128)}, u32[]{:S(2)}, u32[]{:S(2)}) collective-permute-start(f32[64,512]{0,1:T(8,128)S(1)} %collective-permute-done.2), channel_id=1, source_target_pairs={{0,1},{1,2},{2,3},{3,4},{4,5},{5,6},{6,7},{7,0},{8,9},{9,10},{10,1... | collective-permute-start | bytes 393224 | tf_op jit(solution)/shard_map/ppermute | solution.py:37
  209.3 11.1 %collective-permute-start.4 = (f32[64,512]{0,1:T(8,128)}, f32[64,512]{0,1:T(8,128)}, u32[]{:S(2)}, u32[]{:S(2)}) collective-permute-start(f32[64,512]{0,1:T(8,128)} %collective-permute-done.3), channel_id=1, source_target_pairs={{0,1},{1,2},{2,3},{3,4},{4,5},{5,6},{6,7},{7,0},{8,9},{9,10},{10,1... | collective-permute-start | bytes 393224 | tf_op jit(solution)/shard_map/ppermute | solution.py:37
  220.5 10.3 %collective-permute-start.5 = (f32[64,512]{0,1:T(8,128)}, f32[64,512]{0,1:T(8,128)}, u32[]{:S(2)}, u32[]{:S(2)}) collective-permute-start(f32[64,512]{0,1:T(8,128)} %collective-permute-done.4), channel_id=1, source_target_pairs={{0,1},{1,2},{2,3},{3,4},{4,5},{5,6},{6,7},{7,0},{8,9},{9,10},{10,1... | collective-permute-start | bytes 393224 | tf_op jit(solution)/shard_map/ppermute | solution.py:37
  230.7 9.4 %collective-permute-start.6 = (f32[64,512]{0,1:T(8,128)}, f32[64,512]{0,1:T(8,128)}, u32[]{:S(2)}, u32[]{:S(2)}) collective-permute-start(f32[64,512]{0,1:T(8,128)} %collective-permute-done.5), channel_id=1, source_target_pairs={{0,1},{1,2},{2,3},{3,4},{4,5},{5,6},{6,7},{7,0},{8,9},{9,10},{10,1... | collective-permute-start | bytes 393224 | tf_op jit(solution)/shard_map/ppermute | solution.py:37
  255.6 1.0 copy-start.6
  303.3 1.0 copy-start.4
  405.4 6.3 %copy-start.3 = (f32[512,512]{0,1:T(8,128)S(1)}, f32[512,512]{0,1:T(8,128)}, u32[]{:S(2)}) copy-start(f32[512,512]{0,1:T(8,128)} %get-tuple-element.38) | copy-start | bytes 3145732
  405.4 6.7 %copy-start.5 = (f32[512,512]{0,1:T(8,128)S(1)}, f32[512,512]{0,1:T(8,128)}, u32[]{:S(2)}) copy-start(f32[512,512]{0,1:T(8,128)} %get-tuple-element.106) | copy-start | bytes 3145732
  414.4 2.6 copy-start.7
Sparse Core Ops, SparseCore 0:
  18.1 147.8 reduce-scatter.3
